TPU v7x, 32 devices: a whole 2x2x4 slice. The times are simulated.
32 devices in a mesh: ctx: 8 (over y, x, core), wt: 4 (over z).
Axes of the slice: x: 2, y: 2, z: 4, core: 2. Of those that a mesh axis runs over, the one named last changes fastest.
Arguments:
- words: bfloat16 [6144, 512], P(('ctx', 'wt')), may hold values from -6 to 6
- teacher: bfloat16 [6144, 512], P(('ctx', 'wt')), may hold values from -6 to 6
- valid: int32 [6144], P(('ctx', 'wt')), may hold values from 0 to 1, as said below
- lengths: int32 [4], replicated, may hold values from 384 to 3072, as said below
- deal: int32 [32], replicated, may hold values from 0 to 31, as said below
- gain_attn: bfloat16 [512], P('wt'), may hold values from 0.25 to 1.75
- shift_attn: bfloat16 [512], P('wt'), may hold values from -3 to 3
- w_qkv: bfloat16 [512, 1536], P('wt'), may hold values from -0.25 to 0.25
- w_out: bfloat16 [512, 512], P('wt'), may hold values from -2 to 2
- gain_mlp: bfloat16 [512], P('wt'), may hold values from 0.25 to 1.75
- shift_mlp: bfloat16 [512], P('wt'), may hold values from -3 to 3
- w_up: bfloat16 [512, 2048], P('wt'), may hold values from -0.25 to 0.25
- w_down: bfloat16 [2048, 512], P('wt'), may hold values from -0.125 to 0.125
Outputs:
- layer_out: bfloat16 [6144, 512], P(('ctx', 'wt'))
- loss: float32 [], replicated
- grad_words: float32 [6144, 512], P(('ctx', 'wt'))
- grad_gain_attn: float32 [512], P('wt')
- grad_shift_attn: float32 [512], P('wt')
- grad_w_qkv: float32 [512, 1536], P('wt')
- grad_w_out: float32 [512, 512], P('wt')
- grad_gain_mlp: float32 [512], P('wt')
- grad_shift_mlp: float32 [512], P('wt')
- grad_w_up: float32 [512, 2048], P('wt')
- grad_w_down: float32 [2048, 512], P('wt')
Inputs may be any that keep to these rules, and one draw needn't show every extreme that they name: lengths are multiples of 192 that sum to 6144; one sequence has exactly 3072 words. `deal`: each initial block appears once; initial blocks that differ by a multiple of the number of ctx indices lie on the same ctx index. The first word of every dealt block is valid.
All inputs are finite; a program needn't handle non-finite values.
Results may differ from a plain program's by a relative error of at most 0.02.
Values may be sent and summed in bfloat16 or wider, within the bound.
No kernel may reach another device: no remote copies, remote signals or barrier semaphores. Data moves between devices by JAX's collectives and lax.ppermute only.
A program may use at most 128 MiB of HBM per device.

v0:
```python
import jax
import jax.numpy as jnp
from jax import lax
from jax.sharding import PartitionSpec as P

H = 8
HEAD = 64
EPS = 1e-05
LOSS_SCALE = 262144.0


def norm_forward(values, gain_vec, shift_vec):
    center = values - jnp.mean(values, axis=-1, keepdims=True)
    inverse = lax.rsqrt(jnp.mean(center * center, axis=-1, keepdims=True) + EPS)
    unit_rows = center * inverse
    return (unit_rows * gain_vec + shift_vec, unit_rows, inverse)


def norm_backward(upstream, unit_rows, inverse, gain_vec):
    scaled = upstream * gain_vec
    inner_term = jnp.mean(scaled * unit_rows, axis=-1, keepdims=True)
    result = inverse * (scaled - jnp.mean(scaled, axis=-1, keepdims=True) - unit_rows * inner_term)
    return (result, jnp.sum(upstream * unit_rows, axis=0), jnp.sum(upstream, axis=0))


def per_device(
    words,
    teacher,
    valid,
    lengths,
    deal,
    gain_attn,
    shift_attn,
    w_qkv,
    w_out,
    gain_mlp,
    shift_mlp,
    w_up,
    w_down,
):
    ctx_count = lax.axis_size("ctx")
    wt_count = lax.axis_size("wt")
    blk_rows = words.shape[0]
    model_width = words.shape[1]
    head_count = H // wt_count
    col_span = 3 * head_count * HEAD
    group_rows = blk_rows * wt_count
    score_scale = HEAD ** (-0.5)
    qkv_full, out_full, gain_first_raw, shift_first_raw = (
        lax.all_gather(w_qkv, "wt", axis=0, tiled=True),
        lax.all_gather(w_out, "wt", axis=0, tiled=True),
        lax.all_gather(gain_attn, "wt", axis=0, tiled=True),
        lax.all_gather(shift_attn, "wt", axis=0, tiled=True),
    )
    qkv_grouped = qkv_full.reshape(model_width, wt_count, col_span)
    out_grouped = out_full.reshape(wt_count, head_count * HEAD, model_width)
    gain_first = gain_first_raw.astype(jnp.float32)
    shift_first = shift_first_raw.astype(jnp.float32)
    inputs = words.astype(jnp.float32)
    normed_one, unit_first, inverse_first = norm_forward(inputs, gain_first, shift_first)
    packed_first = normed_one.astype(jnp.bfloat16)
    projected = jnp.einsum(
        "rd,dwc->wrc", packed_first, qkv_grouped, preferred_element_type=jnp.float32
    ).astype(jnp.bfloat16)
    head_rows = lax.all_to_all(
        projected.reshape(wt_count, blk_rows * col_span),
        "wt",
        split_axis=0,
        concat_axis=0,
        tiled=True,
    )
    head_rows = head_rows.reshape(group_rows, head_count, 3, HEAD)
    queries = head_rows[:, :, 0]
    own_kv = head_rows[:, :, 1:]
    key_values = own_kv.reshape(group_rows, head_count * 2 * HEAD)
    gathered = lax.all_gather(key_values, "ctx", axis=0, tiled=True).reshape(
        ctx_count, group_rows, head_count, 2, HEAD
    )
    offsets = jnp.arange(blk_rows, dtype=jnp.int32)
    bounds = jnp.cumsum(lengths)
    key_place = (deal[:, None] * blk_rows + offsets[None, :]).reshape(ctx_count, group_rows)
    key_seq = jnp.sum((key_place[:, :, None] >= bounds[None, None, :]).astype(jnp.int32), axis=-1)
    ctx_here = lax.axis_index("ctx")
    query_place = lax.dynamic_index_in_dim(key_place, ctx_here, 0, keepdims=False)
    query_seq = lax.dynamic_index_in_dim(key_seq, ctx_here, 0, keepdims=False)
    live_pieces = jnp.ones((ctx_count,), dtype=bool)
    scan_items = (gathered, key_place, key_seq, live_pieces)

    def scores_of(kv_piece, piece_place, piece_seq):
        raw_scores = (
            jnp.einsum(
                "qhd,khd->hqk", queries, kv_piece[:, :, 0], preferred_element_type=jnp.float32
            )
            * score_scale
        )
        visible = (piece_seq[None, :] == query_seq[:, None]) & (
            piece_place[None, :] <= query_place[:, None]
        )
        return (raw_scores, visible[None])

    def forward_step(carry, item):
        kv_piece, piece_place, piece_seq, live_piece = item
        running_max, running_sum, running_acc = carry
        raw_scores, visible = scores_of(kv_piece, piece_place, piece_seq)
        piece_max = jnp.max(jnp.where(visible, raw_scores, -1e30), axis=-1)
        new_max = jnp.maximum(running_max, piece_max)
        weights = jnp.where(visible, jnp.exp(raw_scores - new_max[..., None]), 0.0)
        factor = jnp.exp(running_max - new_max)
        new_sum = running_sum * factor + jnp.sum(weights, axis=-1)
        new_acc = running_acc * factor.T[:, :, None] + jnp.einsum(
            "hqk,khd->qhd",
            weights.astype(jnp.bfloat16),
            kv_piece[:, :, 1],
            preferred_element_type=jnp.float32,
        )
        return ((new_max, new_sum, new_acc), None)

    start_max = jnp.full((head_count, group_rows), -1e30, jnp.float32)
    start_sum = jnp.zeros((head_count, group_rows), jnp.float32)
    start_acc = jnp.zeros((group_rows, head_count, HEAD), jnp.float32)
    (row_max, row_sum, row_acc), _ = lax.scan(
        forward_step, (start_max, start_sum, start_acc), scan_items
    )
    log_total = row_max + jnp.log(row_sum)
    attended_full = row_acc / row_sum.T[:, :, None]
    attended_heads = attended_full.astype(jnp.bfloat16)
    attended_rows = lax.all_to_all(
        attended_heads.reshape(wt_count, blk_rows * head_count * HEAD),
        "wt",
        split_axis=0,
        concat_axis=0,
        tiled=True,
    ).reshape(wt_count, blk_rows, head_count * HEAD)
    residual_one = inputs + jnp.einsum(
        "wrc,wcd->rd", attended_rows, out_grouped, preferred_element_type=jnp.float32
    )
    up_full, down_full, gain_second_raw, shift_second_raw = (
        lax.all_gather(w_up, "wt", axis=0, tiled=True),
        lax.all_gather(w_down, "wt", axis=0, tiled=True),
        lax.all_gather(gain_mlp, "wt", axis=0, tiled=True),
        lax.all_gather(shift_mlp, "wt", axis=0, tiled=True),
    )
    gain_second = gain_second_raw.astype(jnp.float32)
    shift_second = shift_second_raw.astype(jnp.float32)
    normed_two, unit_second, inverse_second = norm_forward(residual_one, gain_second, shift_second)
    packed_second = normed_two.astype(jnp.bfloat16)
    before_act = jnp.dot(packed_second, up_full, preferred_element_type=jnp.float32)
    activated = jax.nn.gelu(before_act, approximate=False).astype(jnp.bfloat16)
    residual_two = residual_one + jnp.dot(activated, down_full, preferred_element_type=jnp.float32)
    distance = residual_two - teacher.astype(jnp.float32)
    valid_float = valid.astype(jnp.float32)
    count_all, square_all = lax.psum(
        (jnp.sum(valid_float), jnp.sum(valid_float * jnp.sum(distance * distance, axis=-1))),
        ("ctx", "wt"),
    )
    loss_value = square_all / (count_all * model_width)
    grad_two = 2.0 * LOSS_SCALE / (count_all * model_width) * valid_float[:, None] * distance
    grad_branch = grad_two.astype(jnp.bfloat16)
    grad_down = jnp.einsum("rf,rd->fd", activated, grad_branch, preferred_element_type=jnp.float32)
    grad_act = jnp.einsum("rd,fd->rf", grad_branch, down_full, preferred_element_type=jnp.float32)
    _, gelu_back = jax.vjp(lambda hidden_in: jax.nn.gelu(hidden_in, approximate=False), before_act)
    grad_pre = gelu_back(grad_act)[0].astype(jnp.bfloat16)
    grad_up = jnp.einsum("rd,rf->df", packed_second, grad_pre, preferred_element_type=jnp.float32)
    grad_normed_two = jnp.einsum("rf,df->rd", grad_pre, up_full, preferred_element_type=jnp.float32)
    back_two, grad_gain_second, grad_shift_second = norm_backward(
        grad_normed_two, unit_second, inverse_second, gain_second
    )
    grad_one = grad_two + back_two
    grad_attn_out = grad_one.astype(jnp.bfloat16)
    grad_out = jnp.einsum(
        "wrc,rd->wcd", attended_rows, grad_attn_out, preferred_element_type=jnp.float32
    ).reshape(model_width, model_width)
    grad_att_rows = jnp.einsum(
        "rd,wcd->wrc", grad_attn_out, out_grouped, preferred_element_type=jnp.float32
    ).astype(jnp.bfloat16)
    grad_att_heads = lax.all_to_all(
        grad_att_rows.reshape(wt_count, blk_rows * head_count * HEAD),
        "wt",
        split_axis=0,
        concat_axis=0,
        tiled=True,
    ).reshape(group_rows, head_count, HEAD)
    row_delta = jnp.sum(grad_att_heads.astype(jnp.float32) * attended_full, axis=-1).T

    def score_grads(kv_piece, piece_place, piece_seq):
        raw_scores, visible = scores_of(kv_piece, piece_place, piece_seq)
        probs = jnp.where(visible, jnp.exp(raw_scores - log_total[..., None]), 0.0)
        grad_probs = jnp.einsum(
            "qhd,khd->hqk", grad_att_heads, kv_piece[:, :, 1], preferred_element_type=jnp.float32
        )
        return (probs, (probs * (grad_probs - row_delta[..., None])).astype(jnp.bfloat16))

    def grad_step(carry, item):
        kv_piece, piece_place, piece_seq, live_piece = item
        probs, grad_scores = score_grads(kv_piece, piece_place, piece_seq)
        grad_keys = (
            jnp.einsum("hqk,qhd->khd", grad_scores, queries, preferred_element_type=jnp.float32)
            * score_scale
        )
        grad_values = jnp.einsum(
            "hqk,qhd->khd",
            probs.astype(jnp.bfloat16),
            grad_att_heads,
            preferred_element_type=jnp.float32,
        )
        grad_next = carry + jnp.einsum(
            "hqk,khd->qhd", grad_scores, kv_piece[:, :, 0], preferred_element_type=jnp.float32
        )
        return (grad_next, jnp.stack([grad_keys, grad_values], axis=2))

    grad_query_sum, grad_pieces = lax.scan(
        grad_step, jnp.zeros((group_rows, head_count, HEAD), jnp.float32), scan_items
    )
    grad_kv = lax.psum_scatter(
        grad_pieces.reshape(ctx_count * group_rows, head_count * 2 * HEAD).astype(jnp.bfloat16),
        "ctx",
        scatter_dimension=0,
        tiled=True,
    ).astype(jnp.float32)
    grad_kv = grad_kv.astype(jnp.bfloat16).reshape(group_rows, head_count, 2, HEAD)
    grad_queries = (grad_query_sum * score_scale).astype(jnp.bfloat16)
    grad_heads = jnp.concatenate([grad_queries[:, :, None], grad_kv], axis=2)
    grad_rows = lax.all_to_all(
        grad_heads.reshape(wt_count, blk_rows * col_span),
        "wt",
        split_axis=0,
        concat_axis=0,
        tiled=True,
    ).reshape(wt_count, blk_rows, col_span)
    grad_qkv = jnp.einsum(
        "rd,wrc->dwc", packed_first, grad_rows, preferred_element_type=jnp.float32
    ).reshape(model_width, 3 * model_width)
    grad_normed_one = jnp.einsum(
        "wrc,dwc->rd", grad_rows, qkv_grouped, preferred_element_type=jnp.float32
    )
    back_one, grad_gain_first, grad_shift_first = norm_backward(
        grad_normed_one, unit_first, inverse_first, gain_first
    )
    grad_words = grad_one + back_one
    shard_ga, shard_sa, shard_qkv, shard_out, shard_gm, shard_sm, shard_up, shard_down = (
        lax.psum_scatter(
            grad_gain_first.astype(jnp.bfloat16), "wt", scatter_dimension=0, tiled=True
        ).astype(jnp.float32),
        lax.psum_scatter(
            grad_shift_first.astype(jnp.bfloat16), "wt", scatter_dimension=0, tiled=True
        ).astype(jnp.float32),
        lax.psum_scatter(
            grad_qkv.astype(jnp.bfloat16), "wt", scatter_dimension=0, tiled=True
        ).astype(jnp.float32),
        lax.psum_scatter(
            grad_out.astype(jnp.bfloat16), "wt", scatter_dimension=0, tiled=True
        ).astype(jnp.float32),
        lax.psum_scatter(
            grad_gain_second.astype(jnp.bfloat16), "wt", scatter_dimension=0, tiled=True
        ).astype(jnp.float32),
        lax.psum_scatter(
            grad_shift_second.astype(jnp.bfloat16), "wt", scatter_dimension=0, tiled=True
        ).astype(jnp.float32),
        lax.psum_scatter(
            grad_up.astype(jnp.bfloat16), "wt", scatter_dimension=0, tiled=True
        ).astype(jnp.float32),
        lax.psum_scatter(
            grad_down.astype(jnp.bfloat16), "wt", scatter_dimension=0, tiled=True
        ).astype(jnp.float32),
    )
    summed = (
        lax.psum(shard_ga.astype(jnp.bfloat16), "ctx").astype(jnp.float32),
        lax.psum(shard_sa.astype(jnp.bfloat16), "ctx").astype(jnp.float32),
        lax.psum(shard_qkv.astype(jnp.bfloat16), "ctx").astype(jnp.float32),
        lax.psum(shard_out.astype(jnp.bfloat16), "ctx").astype(jnp.float32),
        lax.psum(shard_gm.astype(jnp.bfloat16), "ctx").astype(jnp.float32),
        lax.psum(shard_sm.astype(jnp.bfloat16), "ctx").astype(jnp.float32),
        lax.psum(shard_up.astype(jnp.bfloat16), "ctx").astype(jnp.float32),
        lax.psum(shard_down.astype(jnp.bfloat16), "ctx").astype(jnp.float32),
    )
    return (
        residual_two.astype(jnp.bfloat16),
        loss_value,
        grad_words,
        summed[0],
        summed[1],
        summed[2],
        summed[3],
        summed[4],
        summed[5],
        summed[6],
        summed[7],
    )


def solution(mesh):
    placed = (
        P(("ctx", "wt"), None),
        P(("ctx", "wt"), None),
        P(("ctx", "wt")),
        P(),
        P(),
        P("wt"),
        P("wt"),
        P("wt", None),
        P("wt", None),
        P("wt"),
        P("wt"),
        P("wt", None),
        P("wt", None),
    )
    return jax.shard_map(
        per_device,
        mesh=mesh,
        in_specs=placed,
        out_specs=(
            P(("ctx", "wt"), None),
            P(),
            P(("ctx", "wt"), None),
            P("wt"),
            P("wt"),
            P("wt", None),
            P("wt", None),
            P("wt"),
            P("wt"),
            P("wt", None),
            P("wt", None),
        ),
        check_vma=False,
    )
```

profile of v0, /device:TPU:0, one launch (start us, length us, event | category | flops | bytes accessed | tf_op | source)
XLA Modules:
  0.0 679.7 jit_solution(10840386280325061220)
XLA Ops:
  7.2 2.0 copy.116
  9.3 12.7 %all-gather = bf16[4,1,128]{2,1,0:T(2,128)(2,1)S(1)} all-gather(bf16[1,1,128]{2,1,0:T(2,128)(2,1)} %bitcast.256), channel_id=1, replica_groups=mesh['ctx'=8,'wt'=4] {'wt'}, dimensions={0}, use_global_device_ids=true | all-gather | bytes 1280 | tf_op jit(solution)/shard_map/all_gather | solution.py:52
  22.0 7.8 %all-gather.1 = bf16[4,1,128]{2,1,0:T(2,128)(2,1)S(1)} all-gather(bf16[1,1,128]{2,1,0:T(2,128)(2,1)} %bitcast.257), channel_id=1, replica_groups=mesh['ctx'=8,'wt'=4] {'wt'}, dimensions={0}, use_global_device_ids=true | all-gather | bytes 1280 | tf_op jit(solution)/shard_map/all_gather | solution.py:53
  32.0 18.6 %all-gather.9.cloned.1.call-done = bf16[512,1536]{0,1:T(8,128)(2,1)} async-done(((bf16[128,1536]{0,1:T(8,128)(2,1)}), bf16[512,1536]{0,1:T(8,128)(2,1)}) %all-gather.9.cloned.1.call-update) | async-done | bytes 1572880 | tf_op jit(solution)/shard_map/all_gather | solution.py:50
  50.6 2.1 fusion.40
  53.6 4.4 reduce.16
  58.6 18.8 %all_to_all.40 = bf16[4,2,36864]{2,1,0:T(2,128)(2,1)S(1)} all-to-all(bf16[4,2,36864]{2,1,0:T(2,128)(2,1)S(1)} %reshape.330), channel_id=1, replica_groups=mesh['ctx'=8,'wt'=4] {'wt'}, dimensions={0} | all-to-all | bytes 1179648 | tf_op jit(solution)/shard_map/all_to_all | solution.py:65
  78.0 3.8 reduce.6
  83.7 1.7 copy.119
  90.4 26.7 %all-gather.11.cloned.1.call-done = bf16[6144,256]{0,1:T(8,128)(2,1)} async-done(((bf16[768,256]{0,1:T(8,128)(2,1)}), bf16[6144,256]{0,1:T(8,128)(2,1)}) %all-gather.11.cloned.1.call-update) | async-done | bytes 3145744 | tf_op jit(solution)/shard_map/all_gather | solution.py:76
  117.1 2.8 copy.143
  119.9 2.4 copy.121
  122.3 84.7 %while.28 = (s32[]{:T(128)}, f32[2,768]{1,0:T(2,128)S(1)}, f32[2,768]{1,0:T(2,128)S(1)}, f32[768,2,64]{0,2,1:T(8,128)S(1)}, s32[8,768]{1,0:T(8,128)}, /*index=5*...) while((s32[]{:T(128)}, f32[2,768]{1,0:T(2,128)S(1)}, ...), condition=%wide.region_7.8_spmd.clone, body=%wide.region_4.7_spmd.clone.sunk | while | flops 317039616 | bytes 37675172 | solution.py:121
  124.6 3.2 fusion.119
  127.8 3.8 fusion.123
  135.2 3.2 fusion.119
  138.4 3.8 fusion.123
  145.7 3.2 fusion.119
  148.9 3.8 fusion.123
  156.3 3.2 fusion.119
  159.5 3.8 fusion.123
  166.8 3.2 fusion.119
  170.0 4.1 fusion.123
  177.8 3.2 fusion.119
  181.0 3.8 fusion.123
  188.3 3.2 fusion.119
  191.5 3.9 fusion.123
  198.9 3.2 fusion.119
  202.1 3.8 fusion.123
  210.6 1.9 reduce.17
  213.4 4.5 all-to-all-start.1
  217.9 11.3 %all-gather.2 = bf16[4,1,128]{2,1,0:T(2,128)(2,1)S(1)} all-gather(bf16[1,1,128]{2,1,0:T(2,128)(2,1)S(1)} %bitcast.258), channel_id=1, replica_groups=mesh['ctx'=8,'wt'=4] {'wt'}, dimensions={0}, use_global_device_ids=true | all-gather | bytes 1280 | tf_op jit(solution)/shard_map/all_gather | solution.py:140
  229.2 7.7 %all-gather.3 = bf16[4,1,128]{2,1,0:T(2,128)(2,1)S(1)} all-gather(bf16[1,1,128]{2,1,0:T(2,128)(2,1)S(1)} %bitcast.259), channel_id=1, replica_groups=mesh['ctx'=8,'wt'=4] {'wt'}, dimensions={0}, use_global_device_ids=true | all-gather | bytes 1280 | tf_op jit(solution)/shard_map/all_gather | solution.py:141
  236.9 15.2 %all_gather.31 = bf16[512,512]{1,0:T(8,128)(2,1)S(1)} all-gather(bf16[128,512]{1,0:T(8,128)(2,1)S(1)} %copy-done.20), channel_id=1, replica_groups=mesh['ctx'=8,'wt'=4] {'wt'}, dimensions={0}, use_global_device_ids=true | all-gather | bytes 655360 | tf_op jit(solution)/shard_map/all_gather | solution.py:51
  254.2 6.9 %multiply_convert_fusion = (bf16[192,2048]{1,0:T(8,128)(2,1)}, f32[192,2048]{1,0:T(8,128)}, f32[192,2048]{1,0:T(8,128)}) fusion(bf16[512,2048]{1,0:T(8,128)(2,1)} %all-gather.13.cloned.1.call-done, f32[192,512]{1,0:T(8,128)S(1)} %get-tuple-element.400, f32[512]{0:T(512)S(1)} %bitcast.253, f32[512]{0:T(512)S(1)} %bitcast.249, f32[192]{0:T(256)S(1)} %add_rsqrt_fusion, ...), kind=kOutput, calls=%fused_computation.55 | convolution fusion | flops 428703744 | bytes 6428160 | tf_op jit(solution)/shard_map/dot_general | solution.py:147
  261.1 2.5 multiply_reduce_fusion.3
  264.3 38.9 %all-reduce.4 = (f32[]{:T(128)}, f32[]{:T(128)}) all-reduce(f32[]{:T(128)} %get-tuple-element.324, f32[]{:T(128)} %get-tuple-element.323), channel_id=1, replica_groups=mesh['ctx'=8,'wt'=4] {'ctx','wt'}, use_global_device_ids=true, to_apply=%region_12.13 | all-reduce | flops 2 | bytes 16 | tf_op jit(solution)/shard_map/psum | solution.py:152
  304.0 3.7 add_convert_fusion
  310.5 1.9 reduce.18
  313.3 3.8 all-to-all-start.2
  318.0 5.9 all-to-all-done.2
  328.3 66.9 %while.29 = (s32[]{:T(128)}, f32[768,2,64]{0,2,1:T(8,128)S(1)}, bf16[8,768,2,2,64]{1,4,2,3,0:T(8,128)(2,1)}, bf16[8,768,2,2,64]{1,4,2,3,0:T(8,128)(2,1)}, s32[8,...) while((s32[]{:T(128)}, f32[768,2,64]{0,2,1:T(8,128)S(1)}, ...), condition=%wide.region_19.20_spmd.clone, body=%wide.region_18.19_spmd.clone.sunk | while | flops 769720320 | bytes 28011244 | solution.py:211
  331.5 1.6 fusion.132
  356.6 1.6 fusion.132
  365.0 1.6 fusion.132
  390.1 1.6 fusion.132
  395.1 3.6 copy.129
  398.8 2.6 copy.145
  403.7 2.2 convolution_convert_fusion.1
  407.1 2.1 convolution_convert_fusion
  409.4 38.5 %reduce-scatter.6.cloned.1.call-done = bf16[768,256]{0,1:T(8,128)(2,1)} async-done(((bf16[6144,256]{0,1:T(8,128)(2,1)}), bf16[768,256]{0,1:T(8,128)(2,1)}) %reduce-scatter.6.cloned.1.call-update) | async-done | bytes 393232 | tf_op jit(solution)/shard_map/reduce_scatter | solution.py:214
  450.0 2.1 all_to_all.35
  452.1 5.6 reduce.19
  458.3 23.0 %all_to_all.41 = bf16[4,2,36864]{2,1,0:T(2,128)(2,1)S(1)} all-to-all(bf16[4,2,36864]{2,1,0:T(2,128)(2,1)S(1)} %reshape.336), channel_id=1, replica_groups=mesh['ctx'=8,'wt'=4] {'wt'}, dimensions={0} | all-to-all | bytes 1179648 | tf_op jit(solution)/shard_map/all_to_all | solution.py:223
  481.9 3.8 reduce.9
  486.5 1.9 convolution_convert_fusion.2
  490.3 31.3 %reduce-scatter.12.cloned.1.call-done = bf16[128,2048]{1,0:T(8,128)(2,1)} async-done(((bf16[512,2048]{1,0:T(8,128)(2,1)}), bf16[128,2048]{1,0:T(8,128)(2,1)}) %reduce-scatter.12.cloned.1.call-update) | async-done | bytes 524304 | tf_op jit(solution)/shard_map/reduce_scatter | solution.py:259
  521.7 45.5 %reduce-scatter.14.cloned.1.call-done = bf16[512,512]{1,0:T(8,128)(2,1)} async-done(((bf16[2048,512]{1,0:T(8,128)(2,1)}), bf16[512,512]{1,0:T(8,128)(2,1)}) %reduce-scatter.14.cloned.1.call-update) | async-done | bytes 524304 | tf_op jit(solution)/shard_map/reduce_scatter | solution.py:262
  567.2 37.1 %reduce-scatter.8.cloned.1.call-done = bf16[128,1536]{1,0:T(8,128)(2,1)} async-done(((bf16[512,1536]{1,0:T(8,128)(2,1)}), bf16[128,1536]{1,0:T(8,128)(2,1)}) %reduce-scatter.8.cloned.1.call-update) | async-done | bytes 393232 | tf_op jit(solution)/shard_map/reduce_scatter | solution.py:247
  604.3 2.1 fusion.57
  606.4 9.8 %all-reduce.7 = (bf16[512]{0:T(512)(128)(2,1)S(1)}, bf16[512]{0:T(512)(128)(2,1)S(1)}, bf16[512]{0:T(512)(128)(2,1)S(1)}, bf16[512]{0:T(512)(128)(2,1)S(1)}) all-reduce(bf16[512]{0:T(512)(128)(2,1)S(1)} %get-tuple-element.317, bf16[512]{0:T(512)(128)(2,1)S(1)} %get-tuple-element.322, ...), channel_id=3, replica_groups=mesh['ctx'=8,'wt'=4] {'wt'}, use_global_device_ids=true, to_apply=%region_24.25.clone | all-reduce | flops 2048 | bytes 8192
  616.5 11.9 %all-reduce.5 = (bf16[128]{0:T(256)(128)(2,1)S(1)}, bf16[128]{0:T(256)(128)(2,1)S(1)}, bf16[128]{0:T(256)(128)(2,1)S(1)}, bf16[128]{0:T(256)(128)(2,1)S(1)}) all-reduce(bf16[128]{0:T(256)(128)(2,1)S(1)} %dynamic-slice.1, bf16[128]{0:T(256)(128)(2,1)S(1)} %dynamic-slice.3, ...), channel_id=1, replica_groups=mesh['ctx'=8,'wt'=4] {'ctx'}, use_global_device_ids=true, to_apply=%region_25.26 | all-reduce | flops 512 | bytes 2048 | tf_op jit(solution)/shard_map/psum | solution.py:267
  631.3 35.2 %all-reduce.10.cloned.1.call-done = (bf16[128,1536]{1,0:T(8,128)(2,1)}, bf16[128,512]{1,0:T(8,128)(2,1)}, bf16[128,2048]{1,0:T(8,128)(2,1)}, bf16[512,512]{1,0:T(8,128)(2,1)}) async-done(((bf16[128,1536]{1,0:T(8,128)(2,1)}, bf16[128,512]{1,0:T(8,128)(2,1)}, bf16[128,2048]{1,0:T(8,128)(2,1)}, bf16[512,512]{1,0:T(8,128)(2,1)}), (bf16[128,1536]{1,0:T(8,128)(2,1)}, bf16[128,512]{1,0:T(8,128)(2,1)}, ...) | async-done | bytes 1572880 | tf_op jit(solution)/shard_map/psum | solution.py:269
  666.5 2.2 convert_element_type.184
  (386 shorter events, 129.3 us)
Async XLA Ops:
  7.2 43.5 %copy-start.3 = (bf16[192,512]{1,0:T(8,128)(2,1)S(1)}, bf16[192,512]{1,0:T(8,128)(2,1)}, u32[]{:S(2)}) copy-start(bf16[192,512]{1,0:T(8,128)(2,1)} %param.17) | copy-start | bytes 589828
  7.2 43.4 %all-gather.9.cloned.1.call-start = ((), (), s32[]{:S(2)}) async-start(), calls=%async_computation.9 | async-start | bytes 1966080 | tf_op jit(solution)/shard_map/all_gather | solution.py:50
  9.2 107.9 %all-gather.11.cloned.1.call-start = ((), (), s32[]{:S(2)}) async-start(), calls=%async_computation.10 | async-start | bytes 3538944 | tf_op jit(solution)/shard_map/all_gather | solution.py:76
  22.0 28.6 %copy-start.22 = (f32[4,1,128]{2,1,0:T(1,128)}, f32[4,1,128]{2,1,0:T(1,128)S(1)}, u32[]{:S(2)}) copy-start(f32[4,1,128]{2,1,0:T(1,128)S(1)} %convert_element_type.187) | copy-start | bytes 6148
  29.8 20.8 %copy-start.26 = (f32[4,1,128]{2,1,0:T(1,128)}, f32[4,1,128]{2,1,0:T(1,128)S(1)}, u32[]{:S(2)}) copy-start(f32[4,1,128]{2,1,0:T(1,128)S(1)} %convert_element_type.188) | copy-start | bytes 6148
  30.8 19.8 %copy-start.24 = (f32[192]{0:T(256)}, f32[192]{0:T(256)S(1)}, u32[]{:S(2)}) copy-start(f32[192]{0:T(256)S(1)} %broadcast_multiply_fusion.5) | copy-start | bytes 2308
  32.0 18.6 %copy-start.32 = (f32[192]{0:T(256)}, f32[192]{0:T(256)S(1)}, u32[]{:S(2)}) copy-start(f32[192]{0:T(256)S(1)} %add_rsqrt_fusion.1) | copy-start | bytes 2308
  83.7 3.1 copy-start.46
  83.7 3.5 copy-start.47
  85.4 168.8 %all-gather.13.cloned.1.call-start = ((), (), s32[]{:S(2)}) async-start(), calls=%async_computation.11 | async-start | bytes 2621440 | tf_op jit(solution)/shard_map/all_gather | solution.py:138
  86.1 175.0 %all-gather.15.cloned.1.call-start = ((), (), s32[]{:S(2)}) async-start(), calls=%async_computation.12 | async-start | bytes 2621440 | tf_op jit(solution)/shard_map/all_gather | solution.py:139
  127.8 3.8 copy-start
  138.4 3.8 copy-start
  148.9 3.8 copy-start
  159.5 3.8 copy-start
  170.0 4.3 copy-start
  181.0 3.8 copy-start
  191.5 3.9 copy-start
  202.1 3.8 copy-start
  207.1 3.3 copy-start.17
  210.4 7.5 %copy-start.43 = (bf16[128]{0:T(256)(128)(2,1)S(1)}, bf16[128]{0:T(256)(128)(2,1)}, u32[]{:S(2)}) copy-start(bf16[128]{0:T(256)(128)(2,1)} %param.26) | copy-start | bytes 772
  210.4 18.9 %copy-start.44 = (bf16[128]{0:T(256)(128)(2,1)S(1)}, bf16[128]{0:T(256)(128)(2,1)}, u32[]{:S(2)}) copy-start(bf16[128]{0:T(256)(128)(2,1)} %param.27) | copy-start | bytes 772
  210.4 26.5 %copy-start.20 = (bf16[128,512]{1,0:T(8,128)(2,1)S(1)}, bf16[128,512]{1,0:T(8,128)(2,1)}, u32[]{:S(2)}) copy-start(bf16[128,512]{1,0:T(8,128)(2,1)} %param.25) | copy-start | bytes 393220
  213.4 38.7 %all-to-all-start.1 = ((bf16[4,2,12288]{2,1,0:T(2,128)(2,1)}), bf16[4,2,12288]{2,1,0:T(2,128)(2,1)S(1)}, u32[]{:S(2)}, u32[]{:S(2)}) async-start(bf16[4,2,12288]{2,1,0:T(2,128)(2,1)} %reshape.332), calls=%async_computation.1 | async-start | bytes 393216 | tf_op jit(solution)/shard_map/all_to_all | solution.py:127
  229.2 80.0 %copy-start.28 = (f32[4,1,128]{2,1,0:T(1,128)}, f32[4,1,128]{2,1,0:T(1,128)S(1)}, u32[]{:S(2)}) copy-start(f32[4,1,128]{2,1,0:T(1,128)S(1)} %convert_element_type.189) | copy-start | bytes 6148
  236.9 17.3 %copy-start.36 = (f32[4,1,128]{2,1,0:T(1,128)}, f32[4,1,128]{2,1,0:T(1,128)S(1)}, u32[]{:S(2)}) copy-start(f32[4,1,128]{2,1,0:T(1,128)S(1)} %convert_element_type.190) | copy-start | bytes 6148
  253.5 7.6 %copy-start.8 = (bf16[4,24576]{1,0:T(4,128)(2,1)}, bf16[4,24576]{1,0:T(4,128)(2,1)S(1)}, u32[]{:S(2)}) copy-start(bf16[4,24576]{1,0:T(4,128)(2,1)S(1)} %reduce.7) | copy-start | bytes 589828
  253.9 55.3 %copy-start.1 = (f32[192,512]{1,0:T(8,128)}, f32[192,512]{1,0:T(8,128)S(1)}, u32[]{:S(2)}) copy-start(f32[192,512]{1,0:T(8,128)S(1)} %get-tuple-element.400) | copy-start | bytes 1179652
  253.9 55.3 %copy-start.30 = (f32[192]{0:T(256)}, f32[192]{0:T(256)S(1)}, u32[]{:S(2)}) copy-start(f32[192]{0:T(256)S(1)} %broadcast_multiply_fusion.4) | copy-start | bytes 2308
  254.1 55.1 %copy-start.34 = (f32[192]{0:T(256)}, f32[192]{0:T(256)S(1)}, u32[]{:S(2)}) copy-start(f32[192]{0:T(256)S(1)} %add_rsqrt_fusion) | copy-start | bytes 2308
  254.2 6.9 %copy-start.7 = (bf16[192,512]{1,0:T(8,128)(2,1)S(1)}, bf16[192,512]{1,0:T(8,128)(2,1)}, u32[]{:S(2)}) copy-start(bf16[192,512]{1,0:T(8,128)(2,1)} %param.18) | copy-start | bytes 589828
  261.1 2.6 copy-start.40
  304.0 3.7 copy-start.10
  304.0 3.7 copy-start.45
  307.7 1.5 copy-start.12
  310.1 13.9 %copy-start.4 = (f32[192,512]{1,0:T(8,128)}, f32[192,512]{1,0:T(8,128)S(1)}, u32[]{:S(2)}) copy-start(f32[192,512]{1,0:T(8,128)S(1)} %get-tuple-element.395) | copy-start | bytes 1179652
  310.1 7.2 %copy-start.18 = (f32[2,768]{1,0:T(2,128)S(1)}, f32[2,768]{1,0:T(2,128)}, u32[]{:S(2)}) copy-start(f32[2,768]{1,0:T(2,128)} %copy-done.17) | copy-start | bytes 18436
  313.3 10.5 %all-to-all-start.2 = ((bf16[4,2,12288]{2,1,0:T(2,128)(2,1)}), bf16[4,2,12288]{2,1,0:T(2,128)(2,1)S(1)}, u32[]{:S(2)}, u32[]{:S(2)}) async-start(bf16[4,2,12288]{2,1,0:T(2,128)(2,1)} %reshape.334), calls=%async_computation.2 | async-start | bytes 393216 | tf_op jit(solution)/shard_map/all_to_all | solution.py:176
  317.1 130.7 %reduce-scatter.6.cloned.1.call-start = ((), (), s32[]{:S(2)}) async-start(), calls=%async_computation.13 | async-start | bytes 3538944 | tf_op jit(solution)/shard_map/reduce_scatter | solution.py:214
  330.6 0.9 copy-start.19
  339.0 0.9 copy-start.19
  347.3 0.9 copy-start.19
  355.7 0.9 copy-start.19
  401.4 1.0 copy-start.5
  401.4 1.0 copy-start.9
  401.4 2.2 copy-start.2
  401.4 2.2 copy-start.13
  401.4 2.2 copy-start.29
  401.4 2.2 copy-start.31
  401.4 2.2 copy-start.35
  401.4 2.2 copy-start.37
  401.5 88.9 %reduce-scatter.10.cloned.1.call-start = ((), (), s32[]{:S(2)}) async-start(), calls=%async_computation.15 | async-start | bytes 655360 | tf_op jit(solution)/shard_map/reduce_scatter | solution.py:250
  403.6 118.1 %reduce-scatter.12.cloned.1.call-start = ((), (), s32[]{:S(2)}) async-start(), calls=%async_computation.16 | async-start | bytes 2621440 | tf_op jit(solution)/shard_map/reduce_scatter | solution.py:259
  405.9 1.2 copy-start.6
  405.9 1.3 copy-start.11
  405.9 161.3 %reduce-scatter.14.cloned.1.call-start = ((), (), s32[]{:S(2)}) async-start(), calls=%async_computation.17 | async-start | bytes 2621440 | tf_op jit(solution)/shard_map/reduce_scatter | solution.py:262
  409.3 195.0 %reduce-scatter.8.cloned.1.call-start = ((), (), s32[]{:S(2)}) async-start(), calls=%async_computation.14 | async-start | bytes 1966080 | tf_op jit(solution)/shard_map/reduce_scatter | solution.py:247
  486.5 1.9 copy-start.48
  488.4 178.2 %all-reduce.10.cloned.1.call-start = ((), (), s32[]{:S(2)}) async-start(), calls=%async_computation.18 | async-start | bytes 3145728 | tf_op jit(solution)/shard_map/psum | solution.py:269
  604.3 2.1 copy-start.41
  604.3 2.1 copy-start.42
  666.5 2.2 copy-start.14
  666.5 3.3 copy-start.15
  668.7 2.1 copy-start.21
  (25 other events, 21.8 us)
Sparse Core Ops, SparseCore 0:
  10.2 40.4 all-gather.8
  85.5 31.5 all-gather.10
  118.7 45.9 all-gather.12
  166.1 44.6 all-gather.14
  401.5 46.3 reduce-scatter.5
  450.7 23.8 reduce-scatter.9
  477.0 44.6 reduce-scatter.11
  523.9 43.1 reduce-scatter.13
  569.6 34.5 reduce-scatter.7
  608.1 58.3 all-reduce.9
where the time goes:
time: 687 us; the launch traced here: 680 us
  waiting for transfers between devices  240 us (35%)
  blocking collectives  157 us (23%)
  matrix products  124 us (18%)
  local copies, waits for them, and re-layouts  65.7 us (10%)
  other arithmetic  64.5 us (9%)
  between operations  18.4 us (3%)
  starting transfers between devices  9.25 us (1%)
    reduce_scatter x1, waiting for transfers between devices, per_device(): lax.psum_scatter(grad_down.astype(jnp.bfloat16), 'wt', scatter_dimension=...  45.5 us
    psum x1, blocking collectives, per_device(): lax.psum((jnp.sum(valid_float), jnp.sum(valid_float * jnp.sum(distance *...  38.9 us
    reduce_scatter x1, waiting for transfers between devices, per_device(): lax.psum_scatter(grad_pieces.reshape(ctx_count * group_rows, head_count *...  38.5 us
    reduce_scatter x1, waiting for transfers between devices, per_device(): lax.psum_scatter(grad_qkv.astype(jnp.bfloat16), 'wt', scatter_dimension=0...  37.1 us
    psum x1, waiting for transfers between devices, per_device(): lax.psum(shard_qkv.astype(jnp.bfloat16), 'ctx').astype(jnp.float32)  35.2 us
    dot_general x16, matrix products, scores_of(): jnp.einsum('qhd,khd->hqk', queries, kv_piece[:, :, 0], preferred_element_...  32 us
    reduce_scatter x1, waiting for transfers between devices, per_device(): lax.psum_scatter(grad_up.astype(jnp.bfloat16), 'wt', scatter_dimension=0,...  31.3 us
    dot_general x8, matrix products, forward_step(): jnp.einsum('hqk,khd->qhd', weights.astype(jnp.bfloat16), kv_piece[:, :, 1...  30.9 us
  transfers between devices with their start and end apart: 12, of which 8 were waited for; matrix products, arithmetic and copies ran while one was open for 20% of the time, Pallas kernels for 0%

commit v1 on v0

--- a/solution.py
+++ b/solution.py
@@ -150,8 +150,11 @@
     distance = residual_two - teacher.astype(jnp.float32)
     valid_float = valid.astype(jnp.float32)
     count_all, square_all = lax.psum(
-        (jnp.sum(valid_float), jnp.sum(valid_float * jnp.sum(distance * distance, axis=-1))),
-        ("ctx", "wt"),
+        lax.psum(
+            (jnp.sum(valid_float), jnp.sum(valid_float * jnp.sum(distance * distance, axis=-1))),
+            "wt",
+        ),
+        "ctx",
     )
     loss_value = square_all / (count_all * model_width)
     grad_two = 2.0 * LOSS_SCALE / (count_all * model_width) * valid_float[:, None] * distance

time: 687 us -> 671 us (0.977)
  blocking collectives: 157 us -> 142 us
    psum x1, blocking collectives: 38.9 us -> 11.8 us  [per_device(): lax.psum((jnp.sum(valid_float), jnp.sum(valid_float * jnp.sum(distance *...]
    psum x0 -> x1, blocking collectives: none -> 12.4 us  [per_device(): lax.psum(lax.psum((jnp.sum(valid_float), jnp.sum(valid_float * jnp.sum(di...]
where the time goes in v1:
time: 671 us; the launch traced here: 664 us
  waiting for transfers between devices  239 us (36%)
  blocking collectives  142 us (21%)
  matrix products  124 us (18%)
  local copies, waits for them, and re-layouts  65.8 us (10%)
  other arithmetic  64.5 us (10%)
  between operations  18.3 us (3%)
  starting transfers between devices  9.12 us (1%)
    reduce_scatter x1, waiting for transfers between devices, per_device(): lax.psum_scatter(grad_down.astype(jnp.bfloat16), 'wt', scatter_dimension=...  45.5 us
    reduce_scatter x1, waiting for transfers between devices, per_device(): lax.psum_scatter(grad_qkv.astype(jnp.bfloat16), 'wt', scatter_dimension=0...  37 us
    reduce_scatter x1, waiting for transfers between devices, per_device(): lax.psum_scatter(grad_pieces.reshape(ctx_count * group_rows, head_count *...  36.5 us
    psum x1, waiting for transfers between devices, per_device(): lax.psum(shard_qkv.astype(jnp.bfloat16), 'ctx').astype(jnp.float32)  35.1 us
    dot_general x16, matrix products, scores_of(): jnp.einsum('qhd,khd->hqk', queries, kv_piece[:, :, 0], preferred_element_...  32 us
    reduce_scatter x1, waiting for transfers between devices, per_device(): lax.psum_scatter(grad_up.astype(jnp.bfloat16), 'wt', scatter_dimension=0,...  31.4 us
    dot_general x8, matrix products, forward_step(): jnp.einsum('hqk,khd->qhd', weights.astype(jnp.bfloat16), kv_piece[:, :, 1...  30.9 us
    all_gather x1, waiting for transfers between devices, per_device(): lax.all_gather(key_values, 'ctx', axis=0, tiled=True)  26.7 us
  transfers between devices with their start and end apart: 12, of which 8 were waited for; matrix products, arithmetic and copies ran while one was open for 20% of the time, Pallas kernels for 0%

profile of v1, /device:TPU:0, one launch (start us, length us, event | category | flops | bytes accessed | tf_op | source)
XLA Modules:
  0.0 663.5 jit_solution(9010410010962687493)
XLA Ops:
  7.2 2.0 copy.116
  9.3 12.7 %all-gather = bf16[4,1,128]{2,1,0:T(2,128)(2,1)S(1)} all-gather(bf16[1,1,128]{2,1,0:T(2,128)(2,1)} %bitcast.256), channel_id=1, replica_groups=mesh['ctx'=8,'wt'=4] {'wt'}, dimensions={0}, use_global_device_ids=true | all-gather | bytes 1280 | tf_op jit(solution)/shard_map/all_gather | solution.py:52
  22.0 7.8 %all-gather.1 = bf16[4,1,128]{2,1,0:T(2,128)(2,1)S(1)} all-gather(bf16[1,1,128]{2,1,0:T(2,128)(2,1)} %bitcast.257), channel_id=1, replica_groups=mesh['ctx'=8,'wt'=4] {'wt'}, dimensions={0}, use_global_device_ids=true | all-gather | bytes 1280 | tf_op jit(solution)/shard_map/all_gather | solution.py:53
  32.0 18.6 %all-gather.9.cloned.1.call-done = bf16[512,1536]{0,1:T(8,128)(2,1)} async-done(((bf16[128,1536]{0,1:T(8,128)(2,1)}), bf16[512,1536]{0,1:T(8,128)(2,1)}) %all-gather.9.cloned.1.call-update) | async-done | bytes 1572880 | tf_op jit(solution)/shard_map/all_gather | solution.py:50
  50.6 2.1 fusion.40
  53.6 4.4 reduce.16
  58.6 18.8 %all_to_all.40 = bf16[4,2,36864]{2,1,0:T(2,128)(2,1)S(1)} all-to-all(bf16[4,2,36864]{2,1,0:T(2,128)(2,1)S(1)} %reshape.330), channel_id=1, replica_groups=mesh['ctx'=8,'wt'=4] {'wt'}, dimensions={0} | all-to-all | bytes 1179648 | tf_op jit(solution)/shard_map/all_to_all | solution.py:65
  78.0 3.8 reduce.6
  83.7 1.7 copy.119
  90.4 26.7 %all-gather.11.cloned.1.call-done = bf16[6144,256]{0,1:T(8,128)(2,1)} async-done(((bf16[768,256]{0,1:T(8,128)(2,1)}), bf16[6144,256]{0,1:T(8,128)(2,1)}) %all-gather.11.cloned.1.call-update) | async-done | bytes 3145744 | tf_op jit(solution)/shard_map/all_gather | solution.py:76
  117.1 2.8 copy.143
  119.9 2.4 copy.121
  122.3 84.7 %while.28 = (s32[]{:T(128)}, f32[2,768]{1,0:T(2,128)S(1)}, f32[2,768]{1,0:T(2,128)S(1)}, f32[768,2,64]{0,2,1:T(8,128)S(1)}, s32[8,768]{1,0:T(8,128)}, /*index=5*...) while((s32[]{:T(128)}, f32[2,768]{1,0:T(2,128)S(1)}, ...), condition=%wide.region_7.8_spmd.clone, body=%wide.region_4.7_spmd.clone.sunk | while | flops 317039616 | bytes 37675172 | solution.py:121
  124.6 3.2 fusion.119
  127.8 3.8 fusion.123
  135.2 3.2 fusion.119
  138.4 3.8 fusion.123
  145.7 3.2 fusion.119
  148.9 3.8 fusion.123
  156.3 3.2 fusion.119
  159.5 3.8 fusion.123
  166.8 3.2 fusion.119
  170.0 4.1 fusion.123
  177.8 3.2 fusion.119
  181.0 3.8 fusion.123
  188.3 3.2 fusion.119
  191.5 3.9 fusion.123
  198.9 3.2 fusion.119
  202.1 3.8 fusion.123
  210.6 1.9 reduce.17
  213.4 4.5 all-to-all-start.1
  217.9 11.3 %all-gather.2 = bf16[4,1,128]{2,1,0:T(2,128)(2,1)S(1)} all-gather(bf16[1,1,128]{2,1,0:T(2,128)(2,1)S(1)} %bitcast.258), channel_id=1, replica_groups=mesh['ctx'=8,'wt'=4] {'wt'}, dimensions={0}, use_global_device_ids=true | all-gather | bytes 1280 | tf_op jit(solution)/shard_map/all_gather | solution.py:140
  229.2 7.7 %all-gather.3 = bf16[4,1,128]{2,1,0:T(2,128)(2,1)S(1)} all-gather(bf16[1,1,128]{2,1,0:T(2,128)(2,1)S(1)} %bitcast.259), channel_id=1, replica_groups=mesh['ctx'=8,'wt'=4] {'wt'}, dimensions={0}, use_global_device_ids=true | all-gather | bytes 1280 | tf_op jit(solution)/shard_map/all_gather | solution.py:141
  236.9 15.0 %all_gather.31 = bf16[512,512]{1,0:T(8,128)(2,1)S(1)} all-gather(bf16[128,512]{1,0:T(8,128)(2,1)S(1)} %copy-done.20), channel_id=1, replica_groups=mesh['ctx'=8,'wt'=4] {'wt'}, dimensions={0}, use_global_device_ids=true | all-gather | bytes 655360 | tf_op jit(solution)/shard_map/all_gather | solution.py:51
  254.0 6.9 %multiply_convert_fusion = (bf16[192,2048]{1,0:T(8,128)(2,1)}, f32[192,2048]{1,0:T(8,128)}, f32[192,2048]{1,0:T(8,128)}) fusion(bf16[512,2048]{1,0:T(8,128)(2,1)} %all-gather.13.cloned.1.call-done, f32[192,512]{1,0:T(8,128)S(1)} %get-tuple-element.402, f32[512]{0:T(512)S(1)} %bitcast.253, f32[512]{0:T(512)S(1)} %bitcast.249, f32[192]{0:T(256)S(1)} %add_rsqrt_fusion, ...), kind=kOutput, calls=%fused_computation.55 | convolution fusion | flops 428703744 | bytes 6428160 | tf_op jit(solution)/shard_map/dot_general | solution.py:147
  261.0 2.5 multiply_reduce_fusion.3
  264.1 11.8 %all-reduce.5 = (f32[]{:T(128)}, f32[]{:T(128)}) all-reduce(f32[]{:T(128)} %get-tuple-element.324, f32[]{:T(128)} %get-tuple-element.323), channel_id=1, replica_groups=mesh['ctx'=8,'wt'=4] {'wt'}, use_global_device_ids=true, to_apply=%region_12.13 | all-reduce | flops 2 | bytes 16 | tf_op jit(solution)/shard_map/psum | solution.py:153
  275.9 12.4 %all-reduce.4 = (f32[]{:T(128)}, f32[]{:T(128)}) all-reduce(f32[]{:T(128)} %get-tuple-element.371, f32[]{:T(128)} %get-tuple-element.372), channel_id=1, replica_groups=mesh['ctx'=8,'wt'=4] {'ctx'}, use_global_device_ids=true, to_apply=%region_13.14 | all-reduce | flops 2 | bytes 16 | tf_op jit(solution)/shard_map/psum | solution.py:152
  289.2 3.7 add_convert_fusion
  295.8 1.9 reduce.18
  298.6 3.4 all-to-all-start.2
  303.1 6.6 all-to-all-done.2
  314.1 66.9 %while.29 = (s32[]{:T(128)}, f32[768,2,64]{0,2,1:T(8,128)S(1)}, bf16[8,768,2,2,64]{1,4,2,3,0:T(8,128)(2,1)}, bf16[8,768,2,2,64]{1,4,2,3,0:T(8,128)(2,1)}, s32[8,...) while((s32[]{:T(128)}, f32[768,2,64]{0,2,1:T(8,128)S(1)}, ...), condition=%wide.region_21.22_spmd.clone, body=%wide.region_20.21_spmd.clone.sunk | while | flops 769720320 | bytes 28011244 | solution.py:214
  317.4 1.6 fusion.132
  342.5 1.6 fusion.132
  375.9 1.6 fusion.132
  381.0 3.6 copy.129
  384.7 2.6 copy.145
  389.5 2.2 convolution_convert_fusion.1
  393.0 2.1 convolution_convert_fusion
  395.2 36.5 %reduce-scatter.6.cloned.1.call-done = bf16[768,256]{0,1:T(8,128)(2,1)} async-done(((bf16[6144,256]{0,1:T(8,128)(2,1)}), bf16[768,256]{0,1:T(8,128)(2,1)}) %reduce-scatter.6.cloned.1.call-update) | async-done | bytes 393232 | tf_op jit(solution)/shard_map/reduce_scatter | solution.py:217
  433.8 2.1 all_to_all.35
  436.0 5.6 reduce.19
  442.2 23.0 %all_to_all.41 = bf16[4,2,36864]{2,1,0:T(2,128)(2,1)S(1)} all-to-all(bf16[4,2,36864]{2,1,0:T(2,128)(2,1)S(1)} %reshape.336), channel_id=1, replica_groups=mesh['ctx'=8,'wt'=4] {'wt'}, dimensions={0} | all-to-all | bytes 1179648 | tf_op jit(solution)/shard_map/all_to_all | solution.py:226
  465.8 3.8 reduce.9
  470.3 1.9 convolution_convert_fusion.2
  474.1 31.4 %reduce-scatter.12.cloned.1.call-done = bf16[128,2048]{1,0:T(8,128)(2,1)} async-done(((bf16[512,2048]{1,0:T(8,128)(2,1)}), bf16[128,2048]{1,0:T(8,128)(2,1)}) %reduce-scatter.12.cloned.1.call-update) | async-done | bytes 524304 | tf_op jit(solution)/shard_map/reduce_scatter | solution.py:262
  505.5 45.5 %reduce-scatter.14.cloned.1.call-done = bf16[512,512]{1,0:T(8,128)(2,1)} async-done(((bf16[2048,512]{1,0:T(8,128)(2,1)}), bf16[512,512]{1,0:T(8,128)(2,1)}) %reduce-scatter.14.cloned.1.call-update) | async-done | bytes 524304 | tf_op jit(solution)/shard_map/reduce_scatter | solution.py:265
  551.0 37.0 %reduce-scatter.8.cloned.1.call-done = bf16[128,1536]{1,0:T(8,128)(2,1)} async-done(((bf16[512,1536]{1,0:T(8,128)(2,1)}), bf16[128,1536]{1,0:T(8,128)(2,1)}) %reduce-scatter.8.cloned.1.call-update) | async-done | bytes 393232 | tf_op jit(solution)/shard_map/reduce_scatter | solution.py:250
  588.1 2.1 fusion.57
  590.2 9.8 %all-reduce.8 = (bf16[512]{0:T(512)(128)(2,1)S(1)}, bf16[512]{0:T(512)(128)(2,1)S(1)}, bf16[512]{0:T(512)(128)(2,1)S(1)}, bf16[512]{0:T(512)(128)(2,1)S(1)}) all-reduce(bf16[512]{0:T(512)(128)(2,1)S(1)} %get-tuple-element.317, bf16[512]{0:T(512)(128)(2,1)S(1)} %get-tuple-element.322, ...), channel_id=3, replica_groups=mesh['ctx'=8,'wt'=4] {'wt'}, use_global_device_ids=true, to_apply=%region_26.27.clone | all-reduce | flops 2048 | bytes 8192
  600.3 11.9 %all-reduce.6 = (bf16[128]{0:T(256)(128)(2,1)S(1)}, bf16[128]{0:T(256)(128)(2,1)S(1)}, bf16[128]{0:T(256)(128)(2,1)S(1)}, bf16[128]{0:T(256)(128)(2,1)S(1)}) all-reduce(bf16[128]{0:T(256)(128)(2,1)S(1)} %dynamic-slice.1, bf16[128]{0:T(256)(128)(2,1)S(1)} %dynamic-slice.3, ...), channel_id=1, replica_groups=mesh['ctx'=8,'wt'=4] {'ctx'}, use_global_device_ids=true, to_apply=%region_27.28 | all-reduce | flops 512 | bytes 2048 | tf_op jit(solution)/shard_map/psum | solution.py:270
  615.2 35.1 %all-reduce.11.cloned.1.call-done = (bf16[128,1536]{1,0:T(8,128)(2,1)}, bf16[128,512]{1,0:T(8,128)(2,1)}, bf16[128,2048]{1,0:T(8,128)(2,1)}, bf16[512,512]{1,0:T(8,128)(2,1)}) async-done(((bf16[128,1536]{1,0:T(8,128)(2,1)}, bf16[128,512]{1,0:T(8,128)(2,1)}, bf16[128,2048]{1,0:T(8,128)(2,1)}, bf16[512,512]{1,0:T(8,128)(2,1)}), (bf16[128,1536]{1,0:T(8,128)(2,1)}, bf16[128,512]{1,0:T(8,128)(2,1)}, ...) | async-done | bytes 1572880 | tf_op jit(solution)/shard_map/psum | solution.py:272
  650.4 2.2 convert_element_type.184
  (387 shorter events, 131.2 us)
Async XLA Ops:
  7.2 43.5 %copy-start.3 = (bf16[192,512]{1,0:T(8,128)(2,1)S(1)}, bf16[192,512]{1,0:T(8,128)(2,1)}, u32[]{:S(2)}) copy-start(bf16[192,512]{1,0:T(8,128)(2,1)} %param.17) | copy-start | bytes 589828
  7.2 43.4 %all-gather.9.cloned.1.call-start = ((), (), s32[]{:S(2)}) async-start(), calls=%async_computation.9 | async-start | bytes 1966080 | tf_op jit(solution)/shard_map/all_gather | solution.py:50
  9.2 107.9 %all-gather.11.cloned.1.call-start = ((), (), s32[]{:S(2)}) async-start(), calls=%async_computation.10 | async-start | bytes 3538944 | tf_op jit(solution)/shard_map/all_gather | solution.py:76
  22.0 28.6 %copy-start.22 = (f32[4,1,128]{2,1,0:T(1,128)}, f32[4,1,128]{2,1,0:T(1,128)S(1)}, u32[]{:S(2)}) copy-start(f32[4,1,128]{2,1,0:T(1,128)S(1)} %convert_element_type.187) | copy-start | bytes 6148
  29.8 20.8 %copy-start.26 = (f32[4,1,128]{2,1,0:T(1,128)}, f32[4,1,128]{2,1,0:T(1,128)S(1)}, u32[]{:S(2)}) copy-start(f32[4,1,128]{2,1,0:T(1,128)S(1)} %convert_element_type.188) | copy-start | bytes 6148
  30.8 19.8 %copy-start.24 = (f32[192]{0:T(256)}, f32[192]{0:T(256)S(1)}, u32[]{:S(2)}) copy-start(f32[192]{0:T(256)S(1)} %broadcast_multiply_fusion.5) | copy-start | bytes 2308
  32.0 18.6 %copy-start.32 = (f32[192]{0:T(256)}, f32[192]{0:T(256)S(1)}, u32[]{:S(2)}) copy-start(f32[192]{0:T(256)S(1)} %add_rsqrt_fusion.1) | copy-start | bytes 2308
  83.7 3.1 copy-start.46
  83.7 3.5 copy-start.47
  85.4 168.6 %all-gather.13.cloned.1.call-start = ((), (), s32[]{:S(2)}) async-start(), calls=%async_computation.11 | async-start | bytes 2621440 | tf_op jit(solution)/shard_map/all_gather | solution.py:138
  86.1 174.8 %all-gather.15.cloned.1.call-start = ((), (), s32[]{:S(2)}) async-start(), calls=%async_computation.12 | async-start | bytes 2621440 | tf_op jit(solution)/shard_map/all_gather | solution.py:139
  127.8 3.8 copy-start
  138.4 3.8 copy-start
  148.9 3.8 copy-start
  159.5 3.8 copy-start
  170.0 4.3 copy-start
  181.0 3.8 copy-start
  191.5 3.9 copy-start
  202.1 3.8 copy-start
  207.1 3.3 copy-start.17
  210.4 7.5 %copy-start.43 = (bf16[128]{0:T(256)(128)(2,1)S(1)}, bf16[128]{0:T(256)(128)(2,1)}, u32[]{:S(2)}) copy-start(bf16[128]{0:T(256)(128)(2,1)} %param.26) | copy-start | bytes 772
  210.4 18.9 %copy-start.44 = (bf16[128]{0:T(256)(128)(2,1)S(1)}, bf16[128]{0:T(256)(128)(2,1)}, u32[]{:S(2)}) copy-start(bf16[128]{0:T(256)(128)(2,1)} %param.27) | copy-start | bytes 772
  210.4 26.5 %copy-start.20 = (bf16[128,512]{1,0:T(8,128)(2,1)S(1)}, bf16[128,512]{1,0:T(8,128)(2,1)}, u32[]{:S(2)}) copy-start(bf16[128,512]{1,0:T(8,128)(2,1)} %param.25) | copy-start | bytes 393220
  213.4 38.5 %all-to-all-start.1 = ((bf16[4,2,12288]{2,1,0:T(2,128)(2,1)}), bf16[4,2,12288]{2,1,0:T(2,128)(2,1)S(1)}, u32[]{:S(2)}, u32[]{:S(2)}) async-start(bf16[4,2,12288]{2,1,0:T(2,128)(2,1)} %reshape.332), calls=%async_computation.1 | async-start | bytes 393216 | tf_op jit(solution)/shard_map/all_to_all | solution.py:127
  229.2 65.2 %copy-start.28 = (f32[4,1,128]{2,1,0:T(1,128)}, f32[4,1,128]{2,1,0:T(1,128)S(1)}, u32[]{:S(2)}) copy-start(f32[4,1,128]{2,1,0:T(1,128)S(1)} %convert_element_type.189) | copy-start | bytes 6148
  236.9 17.1 %copy-start.36 = (f32[4,1,128]{2,1,0:T(1,128)}, f32[4,1,128]{2,1,0:T(1,128)S(1)}, u32[]{:S(2)}) copy-start(f32[4,1,128]{2,1,0:T(1,128)S(1)} %convert_element_type.190) | copy-start | bytes 6148
  253.4 7.6 %copy-start.8 = (bf16[4,24576]{1,0:T(4,128)(2,1)}, bf16[4,24576]{1,0:T(4,128)(2,1)S(1)}, u32[]{:S(2)}) copy-start(bf16[4,24576]{1,0:T(4,128)(2,1)S(1)} %reduce.7) | copy-start | bytes 589828
  253.7 40.7 %copy-start.1 = (f32[192,512]{1,0:T(8,128)}, f32[192,512]{1,0:T(8,128)S(1)}, u32[]{:S(2)}) copy-start(f32[192,512]{1,0:T(8,128)S(1)} %get-tuple-element.402) | copy-start | bytes 1179652
  253.8 40.7 %copy-start.30 = (f32[192]{0:T(256)}, f32[192]{0:T(256)S(1)}, u32[]{:S(2)}) copy-start(f32[192]{0:T(256)S(1)} %broadcast_multiply_fusion.4) | copy-start | bytes 2308
  254.0 40.5 %copy-start.34 = (f32[192]{0:T(256)}, f32[192]{0:T(256)S(1)}, u32[]{:S(2)}) copy-start(f32[192]{0:T(256)S(1)} %add_rsqrt_fusion) | copy-start | bytes 2308
  254.0 6.9 %copy-start.7 = (bf16[192,512]{1,0:T(8,128)(2,1)S(1)}, bf16[192,512]{1,0:T(8,128)(2,1)}, u32[]{:S(2)}) copy-start(bf16[192,512]{1,0:T(8,128)(2,1)} %param.18) | copy-start | bytes 589828
  261.0 2.6 copy-start.40
  289.2 3.7 copy-start.10
  289.2 3.7 copy-start.45
  292.9 1.5 copy-start.12
  295.4 14.5 %copy-start.4 = (f32[192,512]{1,0:T(8,128)}, f32[192,512]{1,0:T(8,128)S(1)}, u32[]{:S(2)}) copy-start(f32[192,512]{1,0:T(8,128)S(1)} %get-tuple-element.397) | copy-start | bytes 1179652
  295.4 7.1 %copy-start.18 = (f32[2,768]{1,0:T(2,128)S(1)}, f32[2,768]{1,0:T(2,128)}, u32[]{:S(2)}) copy-start(f32[2,768]{1,0:T(2,128)} %copy-done.17) | copy-start | bytes 18436
  298.6 11.1 %all-to-all-start.2 = ((bf16[4,2,12288]{2,1,0:T(2,128)(2,1)}), bf16[4,2,12288]{2,1,0:T(2,128)(2,1)S(1)}, u32[]{:S(2)}, u32[]{:S(2)}) async-start(bf16[4,2,12288]{2,1,0:T(2,128)(2,1)} %reshape.334), calls=%async_computation.2 | async-start | bytes 393216 | tf_op jit(solution)/shard_map/all_to_all | solution.py:179
  302.0 129.7 %reduce-scatter.6.cloned.1.call-start = ((), (), s32[]{:S(2)}) async-start(), calls=%async_computation.13 | async-start | bytes 3538944 | tf_op jit(solution)/shard_map/reduce_scatter | solution.py:217
  316.5 0.9 copy-start.19
  324.8 0.9 copy-start.19
  333.2 0.9 copy-start.19
  341.5 0.9 copy-start.19
  387.2 1.0 copy-start.5
  387.2 1.0 copy-start.9
  387.3 2.2 copy-start.2
  387.3 2.2 copy-start.13
  387.3 2.2 copy-start.29
  387.3 2.2 copy-start.31
  387.3 2.2 copy-start.35
  387.3 2.2 copy-start.37
  387.3 86.8 %reduce-scatter.10.cloned.1.call-start = ((), (), s32[]{:S(2)}) async-start(), calls=%async_computation.15 | async-start | bytes 655360 | tf_op jit(solution)/shard_map/reduce_scatter | solution.py:253
  389.4 116.1 %reduce-scatter.12.cloned.1.call-start = ((), (), s32[]{:S(2)}) async-start(), calls=%async_computation.16 | async-start | bytes 2621440 | tf_op jit(solution)/shard_map/reduce_scatter | solution.py:262
  391.8 1.2 copy-start.6
  391.8 1.3 copy-start.11
  391.8 159.3 %reduce-scatter.14.cloned.1.call-start = ((), (), s32[]{:S(2)}) async-start(), calls=%async_computation.17 | async-start | bytes 2621440 | tf_op jit(solution)/shard_map/reduce_scatter | solution.py:265
  395.1 192.9 %reduce-scatter.8.cloned.1.call-start = ((), (), s32[]{:S(2)}) async-start(), calls=%async_computation.14 | async-start | bytes 1966080 | tf_op jit(solution)/shard_map/reduce_scatter | solution.py:250
  470.3 1.9 copy-start.48
  472.2 178.2 %all-reduce.11.cloned.1.call-start = ((), (), s32[]{:S(2)}) async-start(), calls=%async_computation.18 | async-start | bytes 3145728 | tf_op jit(solution)/shard_map/psum | solution.py:272
  588.1 2.1 copy-start.41
  588.1 2.1 copy-start.42
  650.4 2.2 copy-start.14
  650.4 3.3 copy-start.15
  652.6 2.1 copy-start.21
  (25 other events, 21.8 us)
Sparse Core Ops, SparseCore 0:
  10.2 40.4 all-gather.8
  85.5 31.5 all-gather.10
  118.7 45.9 all-gather.12
  166.1 44.6 all-gather.14
  387.4 44.2 reduce-scatter.5
  434.5 23.9 reduce-scatter.9
  460.8 44.6 reduce-scatter.11
  507.8 43.1 reduce-scatter.13
  553.5 34.5 reduce-scatter.7
  591.9 58.4 all-reduce.10
